TPU v7x, 256 devices: a whole 4x4x8 slice. The times are simulated.
256 devices in a mesh: dp: 4 (over z_lo), space: 64 (over z_hi, x, y, core).
Axes of the slice: x: 4, y: 4, z: 8 (z_hi: 2, z_lo: 4; z = z_hi * 4 + z_lo), core: 2. Of those that a mesh axis runs over, the one named last changes fastest.
Arguments:
- volumes: bfloat16 [4, 64, 2, 8, 16, 256], P('dp', 'space'), may hold values from -6 to 6
- weight: bfloat16 [256, 6912], P('space', 'dp'), may hold values from -0.078125 to 0.078125
- cotangent: bfloat16 [4, 64, 2, 8, 16, 256], P('dp', 'space'), may hold values from -6 to 6
Outputs:
- features: bfloat16 [4, 64, 2, 8, 16, 256], P('dp', 'space')
- input_grad: bfloat16 [4, 64, 2, 8, 16, 256], P('dp', 'space')
- weight_grad: float32 [256, 6912], P('space', 'dp')
All inputs are finite; a program needn't handle non-finite values.
Results may differ from a plain program's by a relative error of at most 0.0034.
Values may be sent and summed in bfloat16 or wider, within the bound.
No kernel may reach another device: no remote copies, remote signals or barrier semaphores. Data moves between devices by JAX's collectives and lax.ppermute only.
A program may use at most 128 MiB of HBM per device.

v0:
```python
import math
import jax
import jax.numpy as jnp
from jax import lax
from jax.sharding import PartitionSpec as P


def from_behind(block, axis, distance):
    devices = range(lax.axis_size(axis))
    route = [((i - distance) % len(devices), i) for i in devices]
    return lax.ppermute(block, axis, route)


def tap_view(padded, tap, flipped):
    first = tap // 9
    second = tap // 3 % 3
    third = tap % 3
    if flipped:
        first, second, third = (2 - first, 2 - second, 2 - third)
    vols, depth, height, width, chans = padded.shape
    view = padded[
        :, first : first + depth - 2, second : second + height - 2, third : third + width - 2, :
    ]
    return view.reshape(-1, chans)


def per_device(volumes, weight, cotangent):
    own_in = volumes[:, 0]
    own_cot = cotangent[:, 0]
    chans = own_in.shape[-1]
    blocks = lax.axis_size("space")
    grid_cols = min(8, blocks // 2)
    stacked = jnp.stack((own_in, own_cot))
    from_lower = from_behind(stacked[:, :, -1:], "space", grid_cols)
    from_upper = from_behind(stacked[:, :, :1], "space", -grid_cols)
    ext_x = jnp.concatenate((from_lower, stacked, from_upper), axis=2)
    side_lower = from_behind(ext_x[:, :, :, -1:], "space", 1)
    side_upper = from_behind(ext_x[:, :, :, :1], "space", -1)
    ext_xy = jnp.concatenate((side_lower, ext_x, side_upper), axis=3)
    padded = jnp.pad(ext_xy, ((0, 0), (0, 0), (0, 0), (0, 0), (1, 1), (0, 0)))
    in_pad = padded[0]
    cot_pad = padded[1]
    wide = lax.all_gather(weight, "dp", axis=1, tiled=True)
    full_weight = lax.all_gather(wide, "space", axis=0, tiled=True)
    cot_flat = own_cot.reshape(-1, chans)
    cells = cot_flat.shape[0]
    output = jnp.zeros((cells, chans), jnp.float32)
    grad_in = jnp.zeros((cells, chans), jnp.float32)
    grad_blocks = []
    for tap in range(27):
        kernel_tap = full_weight[:, tap * chans : (tap + 1) * chans]
        in_view = tap_view(in_pad, tap, False)
        output = output + lax.dot_general(
            in_view, kernel_tap, (((1,), (1,)), ((), ())), preferred_element_type=jnp.float32
        )
        grad_in = grad_in + jnp.dot(
            tap_view(cot_pad, tap, True), kernel_tap, preferred_element_type=jnp.float32
        )
        grad_blocks.append(
            lax.dot_general(
                cot_flat, in_view, (((0,), (0,)), ((), ())), preferred_element_type=jnp.float32
            )
        )
    features = output.astype(jnp.bfloat16).reshape(volumes.shape)
    input_grad = grad_in.astype(jnp.bfloat16).reshape(volumes.shape)
    voxel_count = cells * lax.axis_size("dp") * blocks
    factor = 1.0 / math.sqrt(voxel_count)
    local_grad = jnp.concatenate(grad_blocks, axis=1) * factor
    partial_rows = lax.psum_scatter(local_grad, "space", scatter_dimension=0, tiled=True)
    weight_grad = lax.psum_scatter(partial_rows, "dp", scatter_dimension=1, tiled=True)
    return (features, input_grad, weight_grad)


def solution(mesh):
    return jax.shard_map(
        per_device,
        mesh=mesh,
        in_specs=(
            P("dp", "space", None, None, None, None),
            P("space", "dp"),
            P("dp", "space", None, None, None, None),
        ),
        out_specs=(
            P("dp", "space", None, None, None, None),
            P("dp", "space", None, None, None, None),
            P("space", "dp"),
        ),
        check_vma=False,
    )
```

profile of v0, /device:TPU:1, one launch (start us, length us, event | category | flops | bytes accessed | tf_op | source)
XLA Modules:
  0.0 1021.1 jit_solution(11820296682975648662)
XLA Ops:
  7.2 0.9 constant_dynamic-update-slice_fusion.1
  8.1 0.9 constant_dynamic-update-slice_fusion
  9.1 10.0 collective-permute-start.1
  19.1 4.8 collective-permute-done.1
  23.9 8.3 collective-permute-done
  32.2 1.7 collective-permute-start.3
  33.9 1.3 collective-permute-start.2
  35.1 11.0 %all-gather = bf16[4,1728,4]{1,2,0:T(4,128)(2,1)S(1)} all-gather(bf16[1,1728,4]{1,2,0:T(4,128)(2,1)} %bitcast.399), channel_id=1, replica_groups=mesh['dp'=4,'space'=64] {'dp'}, dimensions={0}, use_global_device_ids=true | all-gather | bytes 69120 | tf_op jit(solution)/shard_map/all_gather | solution.py:43
  47.0 1.3 dynamic-slice
  50.1 1.5 fusion.92
  58.0 1.5 fusion.91
  59.6 3.4 broadcast_multiply_fusion
  63.2 72.8 %all-gather.4.cloned.1.call-done = bf16[64,4,6912]{2,1,0:T(4,128)(2,1)} async-done(((bf16[1,4,6912]{2,1,0:T(4,128)(2,1)}), bf16[64,4,6912]{2,1,0:T(4,128)(2,1)}) %all-gather.4.cloned.1.call-update) | async-done | bytes 3538960 | tf_op jit(solution)/shard_map/all_gather | solution.py:44
  136.0 5.3 reshape.233
  141.4 1.2 fusion.89
  142.6 1.2 convolution_add_fusion.51
  143.7 1.2 convolution_add_fusion.50
  144.9 1.2 convolution_add_fusion.49
  146.1 1.2 convolution_add_fusion.48
  159.6 775.8 %all-reduce.4.cloned.1.call-done = f32[256,6912]{0,1:T(8,128)} async-done(((f32[256,6912]{0,1:T(8,128)}), f32[256,6912]{0,1:T(8,128)}) %all-reduce.4.cloned.1.call-update) | async-done | bytes 7077904
  935.4 4.8 constant_dynamic-slice_fusion
  940.2 1.9 fusion.29
  942.0 70.4 %reduce-scatter.3.cloned.1.call-done = f32[4,1728]{0,1:T(8,128)} async-done(((f32[4,6912]{0,1:T(8,128)}), f32[4,1728]{0,1:T(8,128)}) %reduce-scatter.3.cloned.1.call-update) | async-done | bytes 27664 | tf_op jit(solution)/shard_map/reduce_scatter | solution.py:70
  1012.5 2.1 copy.10
  (243 shorter events, 19.4 us)
Async XLA Ops:
  7.2 128.8 %all-gather.4.cloned.1.call-start = ((), (), s32[]{:S(2)}) async-start(), calls=%async_computation.2 | async-start | bytes 3594240 | tf_op jit(solution)/shard_map/all_gather | solution.py:44
  9.1 14.8 %collective-permute-start.1 = (bf16[2,1,1,8,16,256]{5,4,3,2,1,0:T(8,128)(2,1)S(1)}, bf16[2,1,1,8,16,256]{5,4,3,2,1,0:T(8,128)(2,1)S(1)}, u32[]{:S(2)}, u32[]{:S(2)}) collective-permute-start(bf16[2,1,1,8,16,256]{5,4,3,2,1,0:T(8,128)(2,1)S(1)} %get-tuple-element.71), channel_id=1, source_target_pairs={{8,0},{9,1},{10,2},{11,3},{12,4},{13,5},{14,6},{15,7},{16,8},{17,9... | collective-permute-start | bytes 393224 | tf_op jit(solution)/shard_map/ppermute | solution.py:11
  19.1 13.1 %collective-permute-start = (bf16[2,1,1,8,16,256]{5,4,3,2,1,0:T(8,128)(2,1)S(1)}, bf16[2,1,1,8,16,256]{5,4,3,2,1,0:T(8,128)(2,1)S(1)}, u32[]{:S(2)}, u32[]{:S(2)}) collective-permute-start(bf16[2,1,1,8,16,256]{5,4,3,2,1,0:T(8,128)(2,1)S(1)} %get-tuple-element.70), channel_id=1, source_target_pairs={{56,0},{57,1},{58,2},{59,3},{60,4},{61,5},{62,6},{63,7},{0,8},{1,9... | collective-permute-start | bytes 393224 | tf_op jit(solution)/shard_map/ppermute | solution.py:11
  32.2 16.7 %collective-permute-start.3 = (bf16[2,1,4,1,16,256]{5,4,3,2,1,0:T(8,128)(2,1)S(1)}, bf16[2,1,4,1,16,256]{5,4,3,2,1,0:T(8,128)(2,1)S(1)}, u32[]{:S(2)}, u32[]{:S(2)}) collective-permute-start(bf16[2,1,4,1,16,256]{5,4,3,2,1,0:T(8,128)(2,1)S(1)} %get-tuple-element.15), channel_id=1, source_target_pairs={{1,0},{2,1},{3,2},{4,3},{5,4},{6,5},{7,6},{8,7},{9,8},{10,9},{11,1... | collective-permute-start | bytes 196616 | tf_op jit(solution)/shard_map/ppermute | solution.py:11
  33.9 15.1 %collective-permute-start.2 = (bf16[2,1,4,1,16,256]{5,4,3,2,1,0:T(8,128)(2,1)S(1)}, bf16[2,1,4,1,16,256]{5,4,3,2,1,0:T(8,128)(2,1)S(1)}, u32[]{:S(2)}, u32[]{:S(2)}) collective-permute-start(bf16[2,1,4,1,16,256]{5,4,3,2,1,0:T(8,128)(2,1)S(1)} %get-tuple-element.14), channel_id=1, source_target_pairs={{63,0},{0,1},{1,2},{2,3},{3,4},{4,5},{5,6},{6,7},{7,8},{8,9},{9,10... | collective-permute-start | bytes 196616 | tf_op jit(solution)/shard_map/ppermute | solution.py:11
  46.9 888.4 %all-reduce.4.cloned.1.call-start = ((), (), s32[]{:S(2)}) async-start(), calls=%async_computation.3 | async-start | bytes 14155776
  50.0 5.5 copy-start.21
  50.0 5.7 copy-start.19
  50.0 5.9 copy-start.17
  50.0 6.2 copy-start.15
  50.0 6.4 copy-start.13
  50.0 6.6 copy-start.11
  50.0 6.8 copy-start.9
  50.0 7.1 copy-start.7
  50.0 7.3 copy-start.5
  50.1 7.5 copy-start.3
  50.1 7.8 copy-start.1
  63.0 949.5 %reduce-scatter.3.cloned.1.call-start = ((), (), s32[]{:S(2)}) async-start(), calls=%async_computation.1 | async-start | bytes 4423680 | tf_op jit(solution)/shard_map/reduce_scatter | solution.py:70
  141.3 6.0 copy-start.44
  141.3 6.2 copy-start.42
  141.3 6.4 copy-start.40
  141.3 6.7 copy-start.38
  141.4 6.9 copy-start.36
  142.6 6.0 copy-start.34
  (59 other events, 162.2 us)
Sparse Core Ops, SparseCore 0:
  47.0 88.9 all-gather.3
  138.7 796.6 all-reduce.3
  940.3 72.1 reduce-scatter.2
where the time goes:
time: 1020 us
  waiting for transfers between devices  932 us (91%)
  matrix products  24.7 us (2%)
  local copies, waits for them, and re-layouts  19.8 us (2%)
  between operations  16.2 us (2%)
  starting transfers between devices  13.3 us (1%)
  blocking collectives  11 us (1%)
    unnamed x4, waiting for transfers between devices  776 us
    all_gather x1, waiting for transfers between devices, per_device(): full_weight = lax.all_gather(wide, 'space', axis=0, tiled=True)  72.8 us
    reduce_scatter x1, waiting for transfers between devices, per_device(): lax.psum_scatter(partial_rows, 'dp', scatter_dimension=1, tiled=True)  70.4 us
  transfers between devices with their start and end apart: 7, of which 5 were waited for; matrix products, arithmetic and copies ran while one was open for 4% of the time, Pallas kernels for 0%

commit v1 on v0

--- a/solution.py
+++ b/solution.py
@@ -41,7 +41,9 @@
     in_pad = padded[0]
     cot_pad = padded[1]
     wide = lax.all_gather(weight, "dp", axis=1, tiled=True)
-    full_weight = lax.all_gather(wide, "space", axis=0, tiled=True)
+    full_weight = jnp.concatenate(
+        lax.all_to_all(jnp.stack([wide] * lax.axis_size("space")), "space", 0, 0), axis=0
+    )
     cot_flat = own_cot.reshape(-1, chans)
     cells = cot_flat.shape[0]
     output = jnp.zeros((cells, chans), jnp.float32)

time: 1020 us -> 980 us (0.961)
  waiting for transfers between devices: 932 us -> 878 us
  starting transfers between devices: 13.3 us -> 24.7 us
    all_gather x1 -> x0, waiting for transfers between devices: 72.8 us -> none  [per_device(): full_weight = lax.all_gather(wide, 'space', axis=0, tiled=True)]
    all_to_all x0 -> x1, waiting for transfers between devices: none -> 71.3 us  [per_device(): lax.all_to_all(jnp.stack([wide] * lax.axis_size('space')), 'space', 0, 0)]
    unnamed x4 -> x3, waiting for transfers between devices: 776 us -> 723 us
    all_to_all x0 -> x1, starting transfers between devices: none -> 11.5 us  [per_device(): lax.all_to_all(jnp.stack([wide] * lax.axis_size('space')), 'space', 0, 0)]
where the time goes in v1:
time: 980 us
  waiting for transfers between devices  878 us (90%)
  starting transfers between devices  24.7 us (3%)
  matrix products  24.7 us (3%)
  local copies, waits for them, and re-layouts  21.2 us (2%)
  between operations  16.5 us (2%)
  blocking collectives  11 us (1%)
    unnamed x3, waiting for transfers between devices  723 us
    all_to_all x1, waiting for transfers between devices, per_device(): lax.all_to_all(jnp.stack([wide] * lax.axis_size('space')), 'space', 0, 0)  71.3 us
    reduce_scatter x1, waiting for transfers between devices, per_device(): lax.psum_scatter(partial_rows, 'dp', scatter_dimension=1, tiled=True)  70.4 us
  transfers between devices with their start and end apart: 7, of which 5 were waited for; matrix products, arithmetic and copies ran while one was open for 4% of the time, Pallas kernels for 0%

profile of v1, /device:TPU:1, one launch (start us, length us, event | category | flops | bytes accessed | tf_op | source)
XLA Modules:
  0.0 979.7 jit_solution(9610871365969354187)
XLA Ops:
  8.1 0.9 constant_dynamic-update-slice_fusion
  9.0 10.0 %collective-permute-start.1 = (bf16[2,1,1,8,16,256]{5,4,3,2,1,0:T(8,128)(2,1)S(1)}, bf16[2,1,1,8,16,256]{5,4,3,2,1,0:T(8,128)(2,1)S(1)}, u32[]{:S(2)}, u32[]{:S(2)}) collective-permute-start(bf16[2,1,1,8,16,256]{5,4,3,2,1,0:T(8,128)(2,1)S(1)} %get-tuple-element.71), channel_id=1, source_target_pairs={{8,0},{9,1},{10,2},{11,3},{12,4},{13,5},{14,6},{15,7},{16,8},{17,9... | collective-permute-start | bytes 393224 | tf_op jit(solution)/shard_map/ppermute | solution.py:11
  19.0 4.8 collective-permute-done.1
  23.8 8.3 collective-permute-done
  32.1 1.7 collective-permute-start.3
  33.8 1.3 collective-permute-start.2
  35.1 11.0 %all-gather = bf16[4,1728,4]{1,2,0:T(4,128)(2,1)S(1)} all-gather(bf16[1,1728,4]{1,2,0:T(4,128)(2,1)} %bitcast.397), channel_id=1, replica_groups=mesh['dp'=4,'space'=64] {'dp'}, dimensions={0}, use_global_device_ids=true | all-gather | bytes 69120 | tf_op jit(solution)/shard_map/all_gather | solution.py:43
  46.2 2.7 stack.5
  48.9 11.5 %all-to-all-start = ((bf16[64,4,6912]{2,1,0:T(4,128)(2,1)}), bf16[64,4,6912]{2,1,0:T(4,128)(2,1)}, u32[]{:S(2)}, u32[]{:S(2)}) async-start(bf16[64,4,6912]{2,1,0:T(4,128)(2,1)} %stack.5), calls=%async_computation | async-start | bytes 7077888 | tf_op jit(solution)/shard_map/all_to_all | solution.py:45
  62.9 1.5 fusion.92
  70.8 3.4 broadcast_multiply_fusion
  74.5 1.5 fusion.91
  76.0 71.3 %all-to-all-done = bf16[64,4,6912]{2,1,0:T(4,128)(2,1)} async-done(((bf16[64,4,6912]{2,1,0:T(4,128)(2,1)}), bf16[64,4,6912]{2,1,0:T(4,128)(2,1)}, u32[]{:S(2)}, u32[]{:S(2)}) %all-to-all-start) | async-done | bytes 3538976 | tf_op jit(solution)/shard_map/all_to_all | solution.py:45
  147.3 5.3 reshape.180
  152.7 1.2 fusion.89
  153.9 1.2 convolution_add_fusion.51
  155.1 1.2 convolution_add_fusion.50
  156.3 1.2 convolution_add_fusion.49
  157.5 1.2 convolution_add_fusion.48
  170.9 722.7 %all-reduce.4.cloned.1.call-done = f32[256,6912]{0,1:T(8,128)} async-done(((f32[256,6912]{0,1:T(8,128)}), f32[256,6912]{0,1:T(8,128)}) %all-reduce.4.cloned.1.call-update) | async-done | bytes 7077904
  893.6 4.8 constant_dynamic-slice_fusion
  898.4 1.9 fusion.29
  900.3 70.4 %reduce-scatter.3.cloned.1.call-done = f32[4,1728]{0,1:T(8,128)} async-done(((f32[4,6912]{0,1:T(8,128)}), f32[4,1728]{0,1:T(8,128)}) %reduce-scatter.3.cloned.1.call-update) | async-done | bytes 27664 | tf_op jit(solution)/shard_map/reduce_scatter | solution.py:72
  970.8 2.1 copy.11
  (245 shorter events, 20.2 us)
Async XLA Ops:
  9.0 14.8 %collective-permute-start.1 = (bf16[2,1,1,8,16,256]{5,4,3,2,1,0:T(8,128)(2,1)S(1)}, bf16[2,1,1,8,16,256]{5,4,3,2,1,0:T(8,128)(2,1)S(1)}, u32[]{:S(2)}, u32[]{:S(2)}) collective-permute-start(bf16[2,1,1,8,16,256]{5,4,3,2,1,0:T(8,128)(2,1)S(1)} %get-tuple-element.71), channel_id=1, source_target_pairs={{8,0},{9,1},{10,2},{11,3},{12,4},{13,5},{14,6},{15,7},{16,8},{17,9... | collective-permute-start | bytes 393224 | tf_op jit(solution)/shard_map/ppermute | solution.py:11
  19.0 13.1 %collective-permute-start = (bf16[2,1,1,8,16,256]{5,4,3,2,1,0:T(8,128)(2,1)S(1)}, bf16[2,1,1,8,16,256]{5,4,3,2,1,0:T(8,128)(2,1)S(1)}, u32[]{:S(2)}, u32[]{:S(2)}) collective-permute-start(bf16[2,1,1,8,16,256]{5,4,3,2,1,0:T(8,128)(2,1)S(1)} %get-tuple-element.70), channel_id=1, source_target_pairs={{56,0},{57,1},{58,2},{59,3},{60,4},{61,5},{62,6},{63,7},{0,8},{1,9... | collective-permute-start | bytes 393224 | tf_op jit(solution)/shard_map/ppermute | solution.py:11
  32.1 29.6 %collective-permute-start.3 = (bf16[2,1,4,1,16,256]{5,4,3,2,1,0:T(8,128)(2,1)S(1)}, bf16[2,1,4,1,16,256]{5,4,3,2,1,0:T(8,128)(2,1)S(1)}, u32[]{:S(2)}, u32[]{:S(2)}) collective-permute-start(bf16[2,1,4,1,16,256]{5,4,3,2,1,0:T(8,128)(2,1)S(1)} %get-tuple-element.15), channel_id=1, source_target_pairs={{1,0},{2,1},{3,2},{4,3},{5,4},{6,5},{7,6},{8,7},{9,8},{10,9},{11,1... | collective-permute-start | bytes 196616 | tf_op jit(solution)/shard_map/ppermute | solution.py:11
  33.8 27.9 %collective-permute-start.2 = (bf16[2,1,4,1,16,256]{5,4,3,2,1,0:T(8,128)(2,1)S(1)}, bf16[2,1,4,1,16,256]{5,4,3,2,1,0:T(8,128)(2,1)S(1)}, u32[]{:S(2)}, u32[]{:S(2)}) collective-permute-start(bf16[2,1,4,1,16,256]{5,4,3,2,1,0:T(8,128)(2,1)S(1)} %get-tuple-element.14), channel_id=1, source_target_pairs={{63,0},{0,1},{1,2},{2,3},{3,4},{4,5},{5,6},{6,7},{7,8},{8,9},{9,10... | collective-permute-start | bytes 196616 | tf_op jit(solution)/shard_map/ppermute | solution.py:11
  48.9 11.5 %copy-start.76 = (u32[256]{0:T(256)S(1)}, u32[256]{0:T(256)}, u32[]{:S(2)}) copy-start(u32[256]{0:T(256)} %constant.12) | copy-start | bytes 3076
  48.9 98.4 %all-to-all-start = ((bf16[64,4,6912]{2,1,0:T(4,128)(2,1)}), bf16[64,4,6912]{2,1,0:T(4,128)(2,1)}, u32[]{:S(2)}, u32[]{:S(2)}) async-start(bf16[64,4,6912]{2,1,0:T(4,128)(2,1)} %stack.5), calls=%async_computation | async-start | bytes 7077888 | tf_op jit(solution)/shard_map/all_to_all | solution.py:45
  60.4 833.2 %all-reduce.4.cloned.1.call-start = ((), (), s32[]{:S(2)}) async-start(), calls=%async_computation.3 | async-start | bytes 14155776
  62.8 5.7 copy-start.19
  62.8 5.9 copy-start.17
  62.8 6.1 copy-start.15
  62.8 6.4 copy-start.13
  62.8 6.6 copy-start.11
  62.8 6.8 copy-start.9
  62.8 7.0 copy-start.7
  62.9 7.3 copy-start.5
  62.9 7.5 copy-start.3
  62.9 7.7 copy-start.1
  74.2 896.5 %reduce-scatter.3.cloned.1.call-start = ((), (), s32[]{:S(2)}) async-start(), calls=%async_computation.2 | async-start | bytes 4423680 | tf_op jit(solution)/shard_map/reduce_scatter | solution.py:72
  152.7 6.0 copy-start.44
  152.7 6.2 copy-start.42
  152.7 6.4 copy-start.40
  152.7 6.7 copy-start.38
  152.7 6.9 copy-start.36
  153.9 6.0 copy-start.34
  (60 other events, 167.5 us)
Sparse Core Ops, SparseCore 0:
  74.4 819.2 all-reduce.3
  898.6 72.1 reduce-scatter.2
